TPU v7x, 32 devices: a whole 2x2x4 slice. The times are simulated.
32 devices in a mesh: groups: 2 (over x), tensor: 4 (over y, core), dp: 4 (over z).
Axes of the slice: x: 2, y: 2, z: 4, core: 2. Of those that a mesh axis runs over, the one named last changes fastest.
Arguments:
- hidden_in: bfloat16 [1024, 8192], P(('groups', 'dp'), 'tensor'), parts along dimension 0, may hold values from -6 to 6
- out_grad: bfloat16 [1024, 8192], P(('groups', 'dp'), 'tensor'), parts along dimension 0, may hold values from -6 to 6
- w_gate_up: bfloat16 [2, 28672, 8192], P(None, ('tensor', 'dp')), may hold values from -0.0625 to 0.0625
- w_down: bfloat16 [28672, 8192], P(('tensor', 'dp')), may hold values from -0.03125 to 0.03125
- feat_proj: bfloat16 [8192, 192], P('tensor'), may hold values from -0.0625 to 0.0625
- unit_proj: bfloat16 [28672, 192], P(('tensor', 'dp')), may hold values from -0.03125 to 0.03125
- precond: float32 [3, 4096, 4096], P(None, ('tensor', 'dp')), may hold values from -20 to 20
Outputs:
- precond_grad: float32 [3, 8, 4096], P(None, 'groups', ('tensor', 'dp')), parts along dimension 1
There are 2 independent parts, one for each index of `groups`. A program takes and returns all parts, laid end to end along the dimension named above; an argument that names none is the same for every part. Nothing has to cross between parts.
All inputs are finite; a program needn't handle non-finite values.
Results may differ from a plain program's by a relative error of at most 0.0029.
Values may be sent and summed in bfloat16 or wider, within the bound.
No kernel may reach another device: no remote copies, remote signals or barrier semaphores. Data moves between devices by JAX's collectives and lax.ppermute only.
A program may use at most 256 MiB of HBM per device.

v0:
```python
import jax
import jax.numpy as jnp
from jax import lax
from jax.sharding import PartitionSpec as P

K = 64
SEQ = 128
contract_last = (((1,), (1,)), ((), ()))


def project_pair(rows_in, rows_out, columns):
    return jnp.concatenate(
        [
            jnp.dot(rows_in, columns[:, : 2 * K], preferred_element_type=jnp.float32),
            jnp.dot(rows_out, columns[:, 2 * K :], preferred_element_type=jnp.float32),
        ],
        axis=1,
    )


def form_sketch(in_side, out_side):
    seq_count = in_side.shape[0] // SEQ
    left_rows = in_side.reshape(seq_count, SEQ, 3, K)
    right_rows = out_side.reshape(seq_count, SEQ, 3, K)
    sketch = jnp.einsum("stwi,stwj->wsij", left_rows, right_rows, precision=lax.Precision.HIGHEST)
    sketch = sketch * SEQ ** (-0.5)
    return sketch.reshape(3, seq_count, K * K)


def local(hidden_in, out_grad, w_gate_up, w_down, feat_proj, unit_proj, precond):
    unit_width = w_down.shape[0]
    model_width = w_down.shape[1]
    w_both = w_gate_up.reshape(2 * unit_width, model_width)
    paired = jnp.stack([hidden_in, out_grad])
    tokens = hidden_in.shape[0] * lax.axis_size("dp")
    columns = lax.all_gather(feat_proj, "tensor", axis=0, tiled=True)
    feat_side = None
    rows_all = lax.all_gather(paired, "dp", axis=1, tiled=True)
    initial = [
        jnp.zeros((tokens, 2 * unit_width), jnp.float32),
        jnp.zeros((tokens, unit_width), jnp.float32),
    ]
    initial.append(jnp.zeros((tokens, 3 * K), jnp.float32))
    pieces = lax.all_gather(rows_all, "tensor", axis=2, tiled=True)
    result = [
        lax.dot_general(pieces[0], w_both, contract_last, preferred_element_type=jnp.float32),
        lax.dot_general(pieces[1], w_down, contract_last, preferred_element_type=jnp.float32),
    ]
    result.append(project_pair(pieces[0], pieces[1], columns))
    folded = tuple(result)
    pre_act = folded[0]
    hid_grad = folded[1]
    feat_side = folded[2]
    gate_pre = pre_act[:, :unit_width]
    up_pre = pre_act[:, unit_width:]
    gate_sig = jax.nn.sigmoid(gate_pre)
    silu_gate = gate_pre * gate_sig
    hidden = (silu_gate * up_pre).astype(jnp.bfloat16)
    gate_grad = (hid_grad * up_pre * gate_sig * (1.0 + gate_pre * (1.0 - gate_sig))).astype(
        jnp.bfloat16
    )
    up_grad = (hid_grad * silu_gate).astype(jnp.bfloat16)
    unit_part = jnp.concatenate(
        [
            jnp.dot(gate_grad, unit_proj[:, :K], preferred_element_type=jnp.float32),
            jnp.dot(up_grad, unit_proj[:, K : 2 * K], preferred_element_type=jnp.float32),
            jnp.dot(hidden, unit_proj[:, 2 * K :], preferred_element_type=jnp.float32),
        ],
        axis=1,
    )
    unit_side = lax.psum(unit_part, ("tensor", "dp"))
    in_side = jnp.concatenate([feat_side[:, : 2 * K], unit_side[:, 2 * K :]], axis=1)
    out_side = jnp.concatenate([unit_side[:, : 2 * K], feat_side[:, 2 * K :]], axis=1)
    sketch = form_sketch(in_side, out_side)
    return jnp.einsum("wrc,wsc->wsr", precond, sketch, precision=lax.Precision.HIGHEST)


def solution(mesh):
    in_specs = (
        P(("groups", "dp"), "tensor"),
        P(("groups", "dp"), "tensor"),
        P(None, ("tensor", "dp"), None),
        P(("tensor", "dp"), None),
        P("tensor", None),
        P(("tensor", "dp"), None),
        P(None, ("tensor", "dp"), None),
    )
    out_specs = P(None, "groups", ("tensor", "dp"))
    return jax.shard_map(local, mesh=mesh, in_specs=in_specs, out_specs=out_specs, check_vma=False)
```

profile of v0, /device:TPU:0, one launch (start us, length us, event | category | flops | bytes accessed | tf_op | source)
XLA Modules:
  0.0 386.8 jit_solution(336281864798562320)
XLA Ops:
  6.5 0.0 all-gather.4.cloned.1.call-start
  6.5 2.3 pad_maximum_fusion
  8.8 0.0 all-gather.4.cloned.1.call-update
  8.8 0.0 all-gather.6.cloned.1.call-start
  8.9 83.6 %all-gather.4.cloned.1.call-done = bf16[2,512,2048]{2,1,0:T(8,128)(2,1)} async-done(((bf16[2,128,2048]{2,1,0:T(8,128)(2,1)}), bf16[2,512,2048]{2,1,0:T(8,128)(2,1)}) %all-gather.4.cloned.1.call-update) | async-done | bytes 4194320 | tf_op jit(solution)/shard_map/all_gather | solution.py:38
  92.4 0.0 all-gather.6.cloned.1.call-update
  92.5 0.0 all-gather.8.cloned.1.call-start
  92.5 0.7 all-gather.8.cloned.1.call-update
  93.2 0.0 all-reduce.2.cloned.1.call-start
  93.3 105.2 %all-gather.6.cloned.1.call-done = bf16[2,512,8192]{2,1,0:T(8,128)(2,1)} async-done(((bf16[2,512,2048]{2,1,0:T(8,128)(2,1)}), bf16[2,512,8192]{2,1,0:T(8,128)(2,1)}) %all-gather.6.cloned.1.call-update) | async-done | bytes 16777232 | tf_op jit(solution)/shard_map/all_gather | solution.py:44
  198.5 0.0 copy-start
  198.5 38.6 %fusion = f32[512,3584]{1,0:T(8,128)} fusion(bf16[3584,8192]{1,0:T(8,128)(2,1)} %bitcast.23, bf16[2,512,8192]{2,1,0:T(8,128)(2,1)} %all-gather.6.cloned.1.call-done), kind=kOutput, calls=%fused_computation.2 | convolution fusion | flops 30064771072 | bytes 74448896 | tf_op jit(solution)/shard_map/dot_general | solution.py:46
  237.1 0.0 copy-done
  237.1 4.3 %fusion.7 = f32[512,64]{0,1:T(8,128)S(1)} fusion(f32[512,3584]{1,0:T(8,128)} %fusion, bf16[1792,192]{0,1:T(8,128)(2,1)S(1)} %copy-done), kind=kOutput, calls=%fused_computation.13 | convolution fusion | flops 122945536 | bytes 7700480 | tf_op jit(solution)/shard_map/dot_general | solution.py:67
  241.3 22.9 %fusion.3 = f32[512,1792]{1,0:T(8,128)} fusion(bf16[1792,8192]{1,0:T(8,128)(2,1)} %param.10, bf16[2,512,8192]{2,1,0:T(8,128)(2,1)} %all-gather.6.cloned.1.call-done), kind=kOutput, calls=%fused_computation.5 | convolution fusion | flops 15032385536 | bytes 41418752 | tf_op jit(solution)/shard_map/dot_general | solution.py:47
  264.3 4.4 %fusion.6 = f32[512,64]{0,1:T(8,128)S(1)} fusion(f32[512,1792]{1,0:T(8,128)} %fusion.3, f32[512,3584]{1,0:T(8,128)} %fusion, bf16[1792,192]{0,1:T(8,128)(2,1)S(1)} %copy-done), kind=kOutput, calls=%fused_computation.12 | convolution fusion | flops 122945536 | bytes 7700480 | tf_op jit(solution)/shard_map/dot_general | solution.py:66
  268.7 0.8 copy-done.1
  269.5 1.0 copy-done.2
  270.5 1.6 fusion.8
  272.1 0.8 pad_maximum_fusion.1
  272.9 0.0 all-reduce.2.cloned.1.call-update
  272.9 0.0 all-gather.8.cloned.1.call-done
  272.9 6.9 %fusion.1 = f32[512,128]{0,1:T(8,128)S(1)} fusion(bf16[2,512,8192]{2,1,0:T(8,128)(2,1)} %all-gather.6.cloned.1.call-done, bf16[8192,192]{0,1:T(8,128)(2,1)} %all-gather.8.cloned.1.call-done), kind=kOutput, calls=%fused_computation.3 | convolution fusion | flops 1073741824 | bytes 10747904 | tf_op jit(solution)/shard_map/dot_general | solution.py:14
  279.8 6.3 %fusion.2 = f32[512,64]{0,1:T(8,128)S(1)} fusion(bf16[2,512,8192]{2,1,0:T(8,128)(2,1)} %all-gather.6.cloned.1.call-done, bf16[8192,192]{0,1:T(8,128)(2,1)} %all-gather.8.cloned.1.call-done), kind=kOutput, calls=%fused_computation.4 | convolution fusion | flops 536870912 | bytes 9568256 | tf_op jit(solution)/shard_map/dot_general | solution.py:15
  286.1 77.3 %all-reduce.2.cloned.1.call-done = f32[512,192]{0,1:T(8,128)} async-done(((f32[512,192]{0,1:T(8,128)}), f32[512,192]{0,1:T(8,128)}) %all-reduce.2.cloned.1.call-update) | async-done | bytes 393232 | tf_op jit(solution)/shard_map/psum | solution.py:71
  363.4 0.9 slice.51
  364.4 0.1 reshape.13
  364.5 1.0 slice.52
  365.5 0.1 reshape.14
  365.7 0.8 convolution_multiply_fusion
  366.4 0.2 reshape.15
  366.6 13.6 %fusion.20 = f32[3,4,256]{2,1,0:T(4,128)} fusion(f32[3,4,4096]{2,1,0:T(4,128)S(1)} %reshape.15, f32[3,256,4096]{2,1,0:T(8,128)} %param.13), kind=kOutput, calls=%fused_computation.29 | convolution fusion | flops 150994944 | bytes 12791808 | tf_op jit(solution)/shard_map/wrc,wsc->wsr/dot_general | solution.py:75
  (4 shorter events, 0.1 us)
Async XLA Ops:
  6.5 85.9 %all-gather.4.cloned.1.call-start = ((), (), s32[]{:S(2)}) async-start(), calls=%async_computation | async-start | bytes 5242880 | tf_op jit(solution)/shard_map/all_gather | solution.py:38
  8.8 189.7 %all-gather.6.cloned.1.call-start = ((), (), s32[]{:S(2)}) async-start(), calls=%async_computation.1 | async-start | bytes 20971520 | tf_op jit(solution)/shard_map/all_gather | solution.py:44
  92.5 180.4 %all-gather.8.cloned.1.call-start = ((), (), s32[]{:S(2)}) async-start(), calls=%async_computation.2 | async-start | bytes 3932160 | tf_op jit(solution)/shard_map/all_gather | solution.py:36
  93.2 270.2 %all-reduce.2.cloned.1.call-start = ((), (), s32[]{:S(2)}) async-start(), calls=%async_computation.3 | async-start | bytes 786432 | tf_op jit(solution)/shard_map/psum | solution.py:71
  198.5 38.6 %copy-start = (bf16[1792,192]{0,1:T(8,128)(2,1)S(1)}, bf16[1792,192]{0,1:T(8,128)(2,1)}, u32[]{:S(2)}) copy-start(bf16[1792,192]{0,1:T(8,128)(2,1)} %param.12) | copy-start | bytes 2064388
  264.3 5.2 %copy-start.1 = (f32[512,3584]{1,0:T(8,128)S(1)}, f32[512,3584]{1,0:T(8,128)}, u32[]{:S(2)}) copy-start(f32[512,3584]{1,0:T(8,128)} %fusion) | copy-start | bytes 22020100
  264.3 6.3 %copy-start.2 = (f32[512,1792]{1,0:T(8,128)S(1)}, f32[512,1792]{1,0:T(8,128)}, u32[]{:S(2)}) copy-start(f32[512,1792]{1,0:T(8,128)} %fusion.3) | copy-start | bytes 11010052
Sparse Core Ops, SparseCore 0:
  9.0 83.4 all-gather.3
  94.0 104.4 all-gather.5
  200.1 28.5 all-gather.7
  273.0 90.3 all-reduce.1
where the time goes:
time: 387 us
  waiting for transfers between devices  267 us (69%)
  matrix products  99.3 us (26%)
  between operations  13.2 us (3%)
  local copies, waits for them, and re-layouts  4.2 us (1%)
    all_gather x1, waiting for transfers between devices, local(): pieces = lax.all_gather(rows_all, 'tensor', axis=2, tiled=True)  105 us
    all_gather x1, waiting for transfers between devices, local(): rows_all = lax.all_gather(paired, 'dp', axis=1, tiled=True)  83.6 us
    psum x1, waiting for transfers between devices, local(): unit_side = lax.psum(unit_part, ('tensor', 'dp'))  77.3 us
    dot_general x1, matrix products, local(): lax.dot_general(pieces[0], w_both, contract_last, preferred_element_type=...  38.6 us
    dot_general x1, matrix products, local(): lax.dot_general(pieces[1], w_down, contract_last, preferred_element_type=...  22.9 us
    dot_general x1, matrix products, local(): jnp.einsum('wrc,wsc->wsr', precond, sketch, precision=lax.Precision.HIGHEST)  13.6 us
  transfers between devices with their start and end apart: 4, of which 3 were waited for; matrix products, arithmetic and copies ran while one was open for 22% of the time, Pallas kernels for 0%

commit v1 on v0

--- a/solution.py
+++ b/solution.py
@@ -68,7 +68,7 @@
         ],
         axis=1,
     )
-    unit_side = lax.psum(unit_part, ("tensor", "dp"))
+    unit_side = lax.psum(lax.psum(unit_part, "dp"), "tensor")
     in_side = jnp.concatenate([feat_side[:, : 2 * K], unit_side[:, 2 * K :]], axis=1)
     out_side = jnp.concatenate([unit_side[:, : 2 * K], feat_side[:, 2 * K :]], axis=1)
     sketch = form_sketch(in_side, out_side)

time: 387 us -> 368 us (0.951)
  waiting for transfers between devices: 267 us -> 248 us
    psum x1 -> x2, waiting for transfers between devices: 77.3 us -> 58.3 us  [local(): unit_side = lax.psum(lax.psum(unit_part, 'dp'), 'tensor')]
  transfers between devices with their start and end apart: 4 -> 5, of which waited for: 3 -> 4; matrix products, arithmetic and copies ran while one was open for 22% -> 23% of each run, Pallas kernels for 0% -> 0%
where the time goes in v1:
time: 368 us
  waiting for transfers between devices  248 us (67%)
  matrix products  99.3 us (27%)
  between operations  13.2 us (4%)
  local copies, waits for them, and re-layouts  4.2 us (1%)
    all_gather x1, waiting for transfers between devices, local(): pieces = lax.all_gather(rows_all, 'tensor', axis=2, tiled=True)  105 us
    all_gather x1, waiting for transfers between devices, local(): rows_all = lax.all_gather(paired, 'dp', axis=1, tiled=True)  83.6 us
    psum x2, waiting for transfers between devices, local(): unit_side = lax.psum(lax.psum(unit_part, 'dp'), 'tensor')  58.3 us
    dot_general x1, matrix products, local(): lax.dot_general(pieces[0], w_both, contract_last, preferred_element_type=...  38.6 us
    dot_general x1, matrix products, local(): lax.dot_general(pieces[1], w_down, contract_last, preferred_element_type=...  22.9 us
    dot_general x1, matrix products, local(): jnp.einsum('wrc,wsc->wsr', precond, sketch, precision=lax.Precision.HIGHEST)  13.6 us
  transfers between devices with their start and end apart: 5, of which 4 were waited for; matrix products, arithmetic and copies ran while one was open for 23% of the time, Pallas kernels for 0%

profile of v1, /device:TPU:0, one launch (start us, length us, event | category | flops | bytes accessed | tf_op | source)
XLA Modules:
  0.0 368.0 jit_solution(13681223250753104398)
XLA Ops:
  6.5 2.3 pad_maximum_fusion
  8.8 0.0 all-gather.4.cloned.1.call-update
  8.8 0.0 all-gather.6.cloned.1.call-start
  8.9 83.6 %all-gather.4.cloned.1.call-done = bf16[2,512,2048]{2,1,0:T(8,128)(2,1)} async-done(((bf16[2,128,2048]{2,1,0:T(8,128)(2,1)}), bf16[2,512,2048]{2,1,0:T(8,128)(2,1)}) %all-gather.4.cloned.1.call-update) | async-done | bytes 4194320 | tf_op jit(solution)/shard_map/all_gather | solution.py:38
  92.4 0.0 all-gather.6.cloned.1.call-update
  92.5 0.0 all-gather.8.cloned.1.call-start
  92.5 0.7 all-gather.8.cloned.1.call-update
  93.2 0.0 all-reduce.3.cloned.1.call-start
  93.3 105.2 %all-gather.6.cloned.1.call-done = bf16[2,512,8192]{2,1,0:T(8,128)(2,1)} async-done(((bf16[2,512,2048]{2,1,0:T(8,128)(2,1)}), bf16[2,512,8192]{2,1,0:T(8,128)(2,1)}) %all-gather.6.cloned.1.call-update) | async-done | bytes 16777232 | tf_op jit(solution)/shard_map/all_gather | solution.py:44
  198.5 38.6 %fusion = f32[512,3584]{1,0:T(8,128)} fusion(bf16[3584,8192]{1,0:T(8,128)(2,1)} %bitcast.23, bf16[2,512,8192]{2,1,0:T(8,128)(2,1)} %all-gather.6.cloned.1.call-done), kind=kOutput, calls=%fused_computation.2 | convolution fusion | flops 30064771072 | bytes 74448896 | tf_op jit(solution)/shard_map/dot_general | solution.py:46
  237.1 4.3 %fusion.7 = f32[512,64]{0,1:T(8,128)S(1)} fusion(f32[512,3584]{1,0:T(8,128)} %fusion, bf16[1792,192]{0,1:T(8,128)(2,1)S(1)} %copy-done), kind=kOutput, calls=%fused_computation.13 | convolution fusion | flops 122945536 | bytes 7700480 | tf_op jit(solution)/shard_map/dot_general | solution.py:67
  241.3 22.9 %fusion.3 = f32[512,1792]{1,0:T(8,128)} fusion(bf16[1792,8192]{1,0:T(8,128)(2,1)} %param.10, bf16[2,512,8192]{2,1,0:T(8,128)(2,1)} %all-gather.6.cloned.1.call-done), kind=kOutput, calls=%fused_computation.5 | convolution fusion | flops 15032385536 | bytes 41418752 | tf_op jit(solution)/shard_map/dot_general | solution.py:47
  264.3 4.4 %fusion.6 = f32[512,64]{0,1:T(8,128)S(1)} fusion(f32[512,1792]{1,0:T(8,128)} %fusion.3, f32[512,3584]{1,0:T(8,128)} %fusion, bf16[1792,192]{0,1:T(8,128)(2,1)S(1)} %copy-done), kind=kOutput, calls=%fused_computation.12 | convolution fusion | flops 122945536 | bytes 7700480 | tf_op jit(solution)/shard_map/dot_general | solution.py:66
  268.7 0.8 copy-done.1
  269.5 1.0 copy-done.2
  270.5 1.6 fusion.8
  272.1 0.8 pad_maximum_fusion.1
  272.9 0.0 all-reduce.3.cloned.1.call-update
  272.9 0.2 all-reduce.5.cloned.1.call-start
  273.1 0.0 all-gather.8.cloned.1.call-done
  273.1 6.9 %fusion.1 = f32[512,128]{0,1:T(8,128)S(1)} fusion(bf16[2,512,8192]{2,1,0:T(8,128)(2,1)} %all-gather.6.cloned.1.call-done, bf16[8192,192]{0,1:T(8,128)(2,1)} %all-gather.8.cloned.1.call-done), kind=kOutput, calls=%fused_computation.3 | convolution fusion | flops 1073741824 | bytes 10747904 | tf_op jit(solution)/shard_map/dot_general | solution.py:14
  280.0 30.1 %all-reduce.3.cloned.1.call-done = f32[512,192]{0,1:T(8,128)} async-done(((f32[512,192]{0,1:T(8,128)}), f32[512,192]{0,1:T(8,128)}) %all-reduce.3.cloned.1.call-update) | async-done | bytes 393232 | tf_op jit(solution)/shard_map/psum | solution.py:71
  310.1 0.0 all-reduce.5.cloned.1.call-update
  310.1 6.3 %fusion.2 = f32[512,64]{0,1:T(8,128)S(1)} fusion(bf16[2,512,8192]{2,1,0:T(8,128)(2,1)} %all-gather.6.cloned.1.call-done, bf16[8192,192]{0,1:T(8,128)(2,1)} %all-gather.8.cloned.1.call-done), kind=kOutput, calls=%fused_computation.4 | convolution fusion | flops 536870912 | bytes 9568256 | tf_op jit(solution)/shard_map/dot_general | solution.py:15
  316.4 28.3 %all-reduce.5.cloned.1.call-done = f32[512,192]{0,1:T(8,128)} async-done(((f32[512,192]{0,1:T(8,128)}), f32[512,192]{0,1:T(8,128)}) %all-reduce.5.cloned.1.call-update) | async-done | bytes 393232 | tf_op jit(solution)/shard_map/psum | solution.py:71
  344.7 0.9 slice.51
  345.6 0.1 reshape.13
  345.8 1.0 slice.52
  346.8 0.1 reshape.14
  346.9 0.7 convolution_multiply_fusion
  347.7 0.2 reshape.15
  347.9 13.6 %fusion.20 = f32[3,4,256]{2,1,0:T(4,128)} fusion(f32[3,4,4096]{2,1,0:T(4,128)S(1)} %reshape.15, f32[3,256,4096]{2,1,0:T(8,128)} %param.13), kind=kOutput, calls=%fused_computation.29 | convolution fusion | flops 150994944 | bytes 12791808 | tf_op jit(solution)/shard_map/wrc,wsc->wsr/dot_general | solution.py:75
  (7 shorter events, 0.1 us)
Async XLA Ops:
  6.5 85.9 %all-gather.4.cloned.1.call-start = ((), (), s32[]{:S(2)}) async-start(), calls=%async_computation | async-start | bytes 5242880 | tf_op jit(solution)/shard_map/all_gather | solution.py:38
  8.8 189.7 %all-gather.6.cloned.1.call-start = ((), (), s32[]{:S(2)}) async-start(), calls=%async_computation.1 | async-start | bytes 20971520 | tf_op jit(solution)/shard_map/all_gather | solution.py:44
  92.5 180.7 %all-gather.8.cloned.1.call-start = ((), (), s32[]{:S(2)}) async-start(), calls=%async_computation.2 | async-start | bytes 3932160 | tf_op jit(solution)/shard_map/all_gather | solution.py:36
  93.2 216.9 %all-reduce.3.cloned.1.call-start = ((), (), s32[]{:S(2)}) async-start(), calls=%async_computation.3 | async-start | bytes 786432 | tf_op jit(solution)/shard_map/psum | solution.py:71
  198.5 38.6 %copy-start = (bf16[1792,192]{0,1:T(8,128)(2,1)S(1)}, bf16[1792,192]{0,1:T(8,128)(2,1)}, u32[]{:S(2)}) copy-start(bf16[1792,192]{0,1:T(8,128)(2,1)} %param.12) | copy-start | bytes 2064388
  264.3 5.2 %copy-start.1 = (f32[512,3584]{1,0:T(8,128)S(1)}, f32[512,3584]{1,0:T(8,128)}, u32[]{:S(2)}) copy-start(f32[512,3584]{1,0:T(8,128)} %fusion) | copy-start | bytes 22020100
  264.3 6.3 %copy-start.2 = (f32[512,1792]{1,0:T(8,128)S(1)}, f32[512,1792]{1,0:T(8,128)}, u32[]{:S(2)}) copy-start(f32[512,1792]{1,0:T(8,128)} %fusion.3) | copy-start | bytes 11010052
  272.9 71.8 %all-reduce.5.cloned.1.call-start = ((), (), s32[]{:S(2)}) async-start(), calls=%async_computation.4 | async-start | bytes 786432 | tf_op jit(solution)/shard_map/psum | solution.py:71
Sparse Core Ops, SparseCore 0:
  9.0 83.4 all-gather.3
  94.0 104.4 all-gather.5
  200.1 28.5 all-gather.7
  273.0 37.0 all-reduce.2
  312.4 32.1 all-reduce.4
